TPU v7x, 32 devices: a whole 2x2x4 slice. The times are simulated.
32 devices in a mesh: dp: 8 (over y, x, core), seq: 4 (over z).
Axes of the slice: x: 2, y: 2, z: 4, core: 2. Of those that a mesh axis runs over, the one named last changes fastest.
Arguments:
- inputs: bfloat16 [8, 1024, 768], P('dp', 'seq'), may hold values from -6 to 6
- d_out: bfloat16 [8, 1024, 768], P('dp', 'seq'), may hold values from -6 to 6
- segments: int32 [8, 1024], P('dp'), may hold values from 0 to 1023, as said below
- buckets: int32 [2048], replicated, may hold values from 0 to 31
- w_query: bfloat16 [768, 768], P(('dp', 'seq')), may hold values from -0.21875 to 0.21875
- w_key: bfloat16 [768, 768], P(('dp', 'seq')), may hold values from -0.21875 to 0.21875
- w_value: bfloat16 [768, 768], P(('dp', 'seq')), may hold values from -0.21875 to 0.21875
- w_out: bfloat16 [768, 768], P(('dp', 'seq')), may hold values from -1.75 to 1.75
- w_gate: bfloat16 [768, 2048], P(('dp', 'seq')), may hold values from -0.21875 to 0.21875
- w_up: bfloat16 [768, 2048], P(('dp', 'seq')), may hold values from -0.21875 to 0.21875
- w_down: bfloat16 [2048, 768], P(('dp', 'seq')), may hold values from -0.1875 to 0.1875
- gain_attn: float32 [768], replicated, may hold values from 0.1 to 1.9
- gain_ffn: float32 [768], replicated, may hold values from 0.1 to 1.9
- bias_table: float32 [32, 12], replicated, may hold values from -4 to 4
Outputs:
- output: bfloat16 [8, 1024, 768], P('dp', 'seq')
- d_inputs: float32 [8, 1024, 768], P('dp', 'seq')
- grad_query: float32 [768, 768], P(('dp', 'seq'))
- grad_key: float32 [768, 768], P(('dp', 'seq'))
- grad_value: float32 [768, 768], P(('dp', 'seq'))
- grad_out: float32 [768, 768], P(('dp', 'seq'))
- grad_gate: float32 [768, 2048], P(('dp', 'seq'))
- grad_up: float32 [768, 2048], P(('dp', 'seq'))
- grad_down: float32 [2048, 768], P(('dp', 'seq'))
- grad_gain_attn: float32 [768], replicated
- grad_gain_ffn: float32 [768], replicated
- grad_table: float32 [32, 12], replicated
Inputs may be any that keep to these rules, and one draw needn't show every extreme that they name: `segments`: each row's label is the index of the last row of its document within the sequence; labels never fall along a sequence, and rows share a document exactly when they share a label.
All inputs are finite; a program needn't handle non-finite values.
Results may differ from a plain program's by a relative error of at most 0.015.
Values may be sent and summed in bfloat16 or wider, within the bound.
No kernel may reach another device: no remote copies, remote signals or barrier semaphores. Data moves between devices by JAX's collectives and lax.ppermute only.
A program may use at most 192 MiB of HBM per device.

v0:
```python
import jax
import jax.numpy as jnp
from jax import lax
from jax.sharding import PartitionSpec as P

EPS = 1e-06
MASKED = -1000000000.0
HIGHEST = lax.Precision.HIGHEST


def norm_rows(values, gain):
    return values * lax.rsqrt(jnp.mean(values * values, axis=-1, keepdims=True) + EPS) * gain


def geglu(gate_act, up_act):
    return jax.nn.gelu(gate_act, approximate=True) * up_act


def matmul(left, right):
    return jnp.dot(left, right, preferred_element_type=jnp.float32)


def left_matmul(left, right):
    return lax.dot_general(
        left, right, (((0,), (0,)), ((), ())), preferred_element_type=jnp.float32
    )


def right_matmul(left, right):
    return lax.dot_general(
        left, right, (((1,), (1,)), ((), ())), preferred_element_type=jnp.float32
    )


def shifted_bias(per_dist, query_count, key_count):
    head_count, width = per_dist.shape
    flipped = per_dist[:, ::-1]
    tiled = jnp.tile(flipped, (1, query_count + 1))[:, : query_count * (width + 1)]
    rows = tiled.reshape(head_count, query_count, width + 1)[:, :, :key_count]
    return rows[:, :, ::-1]


def diagonal_sums(scores):
    head_count, row_count, col_count = scores.shape
    row_width = row_count + col_count
    padded = jnp.concatenate(
        [jnp.zeros((head_count, row_count, row_count), scores.dtype), scores], axis=2
    )
    flat_rows = jnp.concatenate(
        [
            padded.reshape(head_count, row_count * row_width),
            jnp.zeros((head_count, row_count), scores.dtype),
        ],
        axis=1,
    )
    skewed = flat_rows.reshape(head_count, row_count, row_width + 1)
    return jnp.sum(skewed, axis=1)[:, 1:row_width]


def block_parts(
    queries,
    key_heads,
    value_heads,
    seg_query,
    seg_all,
    buckets,
    table,
    first_row,
    blk_index,
    key_block,
):
    query_count = queries.shape[0]
    seq_len = key_heads.shape[0]
    scale = queries.shape[-1] ** (-0.5)
    key_start = blk_index * key_block
    key_blk = lax.dynamic_slice_in_dim(key_heads, key_start, key_block)
    value_blk = lax.dynamic_slice_in_dim(value_heads, key_start, key_block)
    seg_keys = lax.dynamic_slice_in_dim(seg_all, key_start, key_block)
    dist_base = key_start - first_row - query_count + 1 + seq_len
    window = lax.dynamic_slice_in_dim(buckets, dist_base, query_count + key_block - 1)
    onehot = (window[:, None] == jnp.arange(table.shape[0], dtype=jnp.int32)[None, :]).astype(
        jnp.float32
    )
    per_dist = jnp.dot(onehot, table, precision=HIGHEST).T
    bias_blk = shifted_bias(per_dist, query_count, key_block)
    raw_scores = (
        jnp.einsum("qhd,khd->hqk", queries, key_blk, preferred_element_type=jnp.float32) * scale
        + bias_blk
    )
    same_doc = (seg_query[:, None] == seg_keys[None, :])[None]
    weights_exp = jnp.exp(jnp.where(same_doc, raw_scores, MASKED))
    return (key_blk, value_blk, onehot, weights_exp)


def local(
    inputs,
    d_out,
    segments,
    buckets,
    w_query,
    w_key,
    w_value,
    w_out,
    w_gate,
    w_up,
    w_down,
    gain_attn,
    gain_ffn,
    bias_table,
):
    seq_count, row_count, model_width = inputs.shape
    seq_len = segments.shape[1]
    head_count = bias_table.shape[1]
    head_dim = model_width // head_count
    key_block = min(512, seq_len)
    block_count = seq_len // key_block
    token_count = seq_count * row_count
    scale = head_dim ** (-0.5)
    first_row = lax.axis_index("seq") * row_count
    blk_ids = jnp.arange(block_count, dtype=jnp.int32)
    gathered = (
        lax.all_gather(w_query, ("dp", "seq"), axis=0, tiled=True),
        lax.all_gather(w_key, ("dp", "seq"), axis=0, tiled=True),
        lax.all_gather(w_value, ("dp", "seq"), axis=0, tiled=True),
        lax.all_gather(w_out, ("dp", "seq"), axis=0, tiled=True),
        lax.all_gather(w_gate, ("dp", "seq"), axis=0, tiled=True),
        lax.all_gather(w_up, ("dp", "seq"), axis=0, tiled=True),
        lax.all_gather(w_down, ("dp", "seq"), axis=0, tiled=True),
    )
    full_query, full_key, full_value, full_out, full_gate, full_up, full_down = gathered
    flat_in = inputs.reshape(token_count, model_width).astype(jnp.float32)
    normed = norm_rows(flat_in, gain_attn).astype(jnp.bfloat16)
    queries = matmul(normed, full_query).astype(jnp.bfloat16)
    key_rows = (
        matmul(normed, full_key).astype(jnp.bfloat16).reshape(seq_count, row_count, model_width)
    )
    value_rows = (
        matmul(normed, full_value).astype(jnp.bfloat16).reshape(seq_count, row_count, model_width)
    )
    key_all, value_all = (
        lax.all_gather(key_rows, "seq", axis=1, tiled=True),
        lax.all_gather(value_rows, "seq", axis=1, tiled=True),
    )
    query_heads = queries.reshape(seq_count, row_count, head_count, head_dim)
    key_heads = key_all.reshape(seq_count, seq_len, head_count, head_dim)
    value_heads = value_all.reshape(seq_count, seq_len, head_count, head_dim)
    seg_queries = lax.dynamic_slice_in_dim(segments, first_row, row_count, axis=1)

    def attend(packed):
        query_one, key_one, value_one, seg_query, seg_all = packed

        def step(state_in, blk_index):
            totals, summed = state_in
            _, value_blk, _, weights_exp = block_parts(
                query_one,
                key_one,
                value_one,
                seg_query,
                seg_all,
                buckets,
                bias_table,
                first_row,
                blk_index,
                key_block,
            )
            summed = summed + jnp.einsum(
                "hqk,khd->qhd",
                weights_exp.astype(jnp.bfloat16),
                value_blk,
                preferred_element_type=jnp.float32,
            )
            totals = totals + jnp.sum(weights_exp, axis=-1)
            return ((totals, summed), None)

        start_state = (
            jnp.zeros((head_count, row_count), jnp.float32),
            jnp.zeros((row_count, head_count, head_dim), jnp.float32),
        )
        (totals, summed), _ = lax.scan(step, start_state, blk_ids)
        return (summed / jnp.transpose(totals)[:, :, None], totals)

    attn_f32, totals_all = lax.map(
        attend, (query_heads, key_heads, value_heads, seg_queries, segments)
    )
    attn_rows = attn_f32.reshape(token_count, model_width).astype(jnp.bfloat16)
    mixed_rows = flat_in + matmul(attn_rows, full_out)
    normed_two = norm_rows(mixed_rows, gain_ffn).astype(jnp.bfloat16)
    gate_act = matmul(normed_two, full_gate)
    up_act = matmul(normed_two, full_up)
    hidden = geglu(gate_act, up_act).astype(jnp.bfloat16)
    result = mixed_rows + matmul(hidden, full_down)
    output = result.astype(jnp.bfloat16).reshape(seq_count, row_count, model_width)
    back_weights = (
        lax.all_gather(w_query, ("dp", "seq"), axis=0, tiled=True),
        lax.all_gather(w_key, ("dp", "seq"), axis=0, tiled=True),
        lax.all_gather(w_value, ("dp", "seq"), axis=0, tiled=True),
        lax.all_gather(w_out, ("dp", "seq"), axis=0, tiled=True),
        lax.all_gather(w_gate, ("dp", "seq"), axis=0, tiled=True),
        lax.all_gather(w_up, ("dp", "seq"), axis=0, tiled=True),
        lax.all_gather(w_down, ("dp", "seq"), axis=0, tiled=True),
    )
    back_query, back_key, back_value, back_out, back_gate, back_up, back_down = back_weights
    d_res = d_out.reshape(token_count, model_width)
    grad_down = left_matmul(hidden, d_res)
    d_hidden = right_matmul(d_res, back_down)
    _, geglu_back = jax.vjp(geglu, gate_act, up_act)
    d_gate, d_up = geglu_back(d_hidden)
    d_gate = d_gate.astype(jnp.bfloat16)
    d_up = d_up.astype(jnp.bfloat16)
    grad_gate = left_matmul(normed_two, d_gate)
    grad_up = left_matmul(normed_two, d_up)
    d_normed_two = right_matmul(d_gate, back_gate) + right_matmul(d_up, back_up)
    _, norm_two_back = jax.vjp(norm_rows, mixed_rows, gain_ffn)
    d_mixed_norm, grad_gain_ffn = norm_two_back(d_normed_two)
    d_mixed = d_res.astype(jnp.float32) + d_mixed_norm
    d_branch = d_mixed.astype(jnp.bfloat16)
    grad_out = left_matmul(attn_rows, d_branch)
    d_attn = right_matmul(d_branch, back_out).reshape(seq_count, row_count, head_count, head_dim)
    totals_rows = jnp.transpose(totals_all, (0, 2, 1))
    d_unnorm_all = (d_attn / totals_rows[:, :, :, None]).astype(jnp.bfloat16)
    correction_all = -jnp.sum(d_attn * attn_f32, axis=-1) / totals_rows

    def attend_back(packed):
        query_one, key_one, value_one, seg_query, seg_all, d_unnorm, corr_rows = packed
        correction = jnp.transpose(corr_rows)

        def step(state_in, blk_index):
            d_query, d_table = state_in
            key_blk, value_blk, onehot, weights_exp = block_parts(
                query_one,
                key_one,
                value_one,
                seg_query,
                seg_all,
                buckets,
                bias_table,
                first_row,
                blk_index,
                key_block,
            )
            d_prob = jnp.einsum(
                "qhd,khd->hqk", d_unnorm, value_blk, preferred_element_type=jnp.float32
            )
            d_raw = (weights_exp * (d_prob + correction[:, :, None])).astype(jnp.bfloat16)
            d_query = (
                d_query
                + jnp.einsum("hqk,khd->qhd", d_raw, key_blk, preferred_element_type=jnp.float32)
                * scale
            )
            d_table = d_table + jnp.dot(
                diagonal_sums(d_raw.astype(jnp.float32)), onehot, precision=HIGHEST
            )
            d_key = (
                jnp.einsum("hqk,qhd->khd", d_raw, query_one, preferred_element_type=jnp.float32)
                * scale
            )
            d_value = jnp.einsum(
                "hqk,qhd->khd",
                weights_exp.astype(jnp.bfloat16),
                d_unnorm,
                preferred_element_type=jnp.float32,
            )
            return ((d_query, d_table), (d_key, d_value))

        start_state = (
            jnp.zeros((row_count, head_count, head_dim), jnp.float32),
            jnp.zeros((head_count, bias_table.shape[0]), jnp.float32),
        )
        (d_query, d_table), key_parts = lax.scan(step, start_state, blk_ids)
        d_key, d_value = key_parts
        return (
            d_query,
            d_table,
            d_key.reshape(seq_len, model_width),
            d_value.reshape(seq_len, model_width),
        )

    back_inputs = (
        query_heads,
        key_heads,
        value_heads,
        seg_queries,
        segments,
        d_unnorm_all,
        correction_all,
    )
    d_query_all, d_table_all, d_key_all, d_value_all = lax.map(attend_back, back_inputs)
    d_key_own, d_value_own = (
        lax.psum_scatter(
            d_key_all.astype(jnp.bfloat16), "seq", scatter_dimension=1, tiled=True
        ).astype(jnp.float32),
        lax.psum_scatter(
            d_value_all.astype(jnp.bfloat16), "seq", scatter_dimension=1, tiled=True
        ).astype(jnp.float32),
    )
    d_query_b = d_query_all.reshape(token_count, model_width).astype(jnp.bfloat16)
    d_key_b = d_key_own.reshape(token_count, model_width).astype(jnp.bfloat16)
    d_value_b = d_value_own.reshape(token_count, model_width).astype(jnp.bfloat16)
    grad_query = left_matmul(normed, d_query_b)
    grad_key = left_matmul(normed, d_key_b)
    grad_value = left_matmul(normed, d_value_b)
    d_normed = (
        right_matmul(d_query_b, back_query)
        + right_matmul(d_key_b, back_key)
        + right_matmul(d_value_b, back_value)
    )
    _, norm_one_back = jax.vjp(norm_rows, flat_in, gain_attn)
    d_in_norm, grad_gain_attn = norm_one_back(d_normed)
    d_inputs = (d_mixed + d_in_norm).reshape(seq_count, row_count, model_width)
    owned = (
        lax.psum_scatter(grad_query, ("dp", "seq"), scatter_dimension=0, tiled=True),
        lax.psum_scatter(grad_key, ("dp", "seq"), scatter_dimension=0, tiled=True),
        lax.psum_scatter(grad_value, ("dp", "seq"), scatter_dimension=0, tiled=True),
        lax.psum_scatter(grad_out, ("dp", "seq"), scatter_dimension=0, tiled=True),
        lax.psum_scatter(grad_gate, ("dp", "seq"), scatter_dimension=0, tiled=True),
        lax.psum_scatter(grad_up, ("dp", "seq"), scatter_dimension=0, tiled=True),
        lax.psum_scatter(grad_down, ("dp", "seq"), scatter_dimension=0, tiled=True),
    )
    table_local = jnp.transpose(jnp.sum(d_table_all, axis=0))
    gain_one, gain_two, table_grad = lax.psum(
        (grad_gain_attn, grad_gain_ffn, table_local), ("dp", "seq")
    )
    return (
        output,
        d_inputs,
        owned[0],
        owned[1],
        owned[2],
        owned[3],
        owned[4],
        owned[5],
        owned[6],
        gain_one,
        gain_two,
        table_grad,
    )


def solution(mesh):
    return jax.shard_map(
        local,
        mesh=mesh,
        in_specs=(
            P("dp", "seq", None),
            P("dp", "seq", None),
            P("dp", None),
            P(),
            P(("dp", "seq"), None),
            P(("dp", "seq"), None),
            P(("dp", "seq"), None),
            P(("dp", "seq"), None),
            P(("dp", "seq"), None),
            P(("dp", "seq"), None),
            P(("dp", "seq"), None),
            P(),
            P(),
            P(),
        ),
        out_specs=(
            P("dp", "seq", None),
            P("dp", "seq", None),
            P(("dp", "seq"), None),
            P(("dp", "seq"), None),
            P(("dp", "seq"), None),
            P(("dp", "seq"), None),
            P(("dp", "seq"), None),
            P(("dp", "seq"), None),
            P(("dp", "seq"), None),
            P(),
            P(),
            P(),
        ),
        check_vma=False,
    )
```

profile of v0, /device:TPU:0, one launch (start us, length us, event | category | flops | bytes accessed | tf_op | source)
XLA Modules:
  0.0 1757.2 jit_solution(12982344528251555989)
XLA Ops:
  10.7 57.0 %all-gather.16.cloned.1.call-done = bf16[768,768]{1,0:T(8,128)(2,1)} async-done(((bf16[24,768]{1,0:T(8,128)(2,1)}), bf16[768,768]{1,0:T(8,128)(2,1)}) %all-gather.16.cloned.1.call-update) | async-done | bytes 1179664 | tf_op jit(solution)/shard_map/all_gather | solution.py:124
  70.4 53.1 %all-gather.12.cloned.1.call-done = bf16[768,768]{1,0:T(8,128)(2,1)} async-done(((bf16[24,768]{1,0:T(8,128)(2,1)}), bf16[768,768]{1,0:T(8,128)(2,1)}) %all-gather.12.cloned.1.call-update) | async-done | bytes 1179664 | tf_op jit(solution)/shard_map/all_gather | solution.py:123
  130.3 49.1 %all-gather.14.cloned.1.call-done = bf16[768,768]{1,0:T(8,128)(2,1)} async-done(((bf16[24,768]{1,0:T(8,128)(2,1)}), bf16[768,768]{1,0:T(8,128)(2,1)}) %all-gather.14.cloned.1.call-update) | async-done | bytes 1179664 | tf_op jit(solution)/shard_map/all_gather | solution.py:122
  181.4 35.5 %all-gather.28.cloned.1.call-done = bf16[1024,768]{1,0:T(8,128)(2,1)} async-done(((bf16[256,768]{1,0:T(8,128)(2,1)}), bf16[1024,768]{1,0:T(8,128)(2,1)}) %all-gather.28.cloned.1.call-update) | async-done | bytes 1572880 | tf_op jit(solution)/shard_map/all_gather | solution.py:142
  218.6 36.3 %all-gather.26.cloned.1.call-done = bf16[1024,768]{1,0:T(8,128)(2,1)} async-done(((bf16[256,768]{1,0:T(8,128)(2,1)}), bf16[1024,768]{1,0:T(8,128)(2,1)}) %all-gather.26.cloned.1.call-update) | async-done | bytes 1572880 | tf_op jit(solution)/shard_map/all_gather | solution.py:141
  257.1 241.5 %while.60 = (s32[]{:T(128)}, f32[12,256]{1,0:T(8,128)S(1)}, f32[256,12,64]{0,2,1:T(8,128)}, s32[256]{0:T(256)}, s32[2]{0:T(128)}, /*index=5*/s32[1024]{0:T(1024)...) while((s32[]{:T(128)}, f32[12,256]{1,0:T(8,128)S(1)}, ...), condition=%wide.region_3.4_spmd.clone, body=%wide.region_1.3_spmd.clone.sunk | while | flops 414603776 | bytes 133137936 | solution.py:179
  273.0 14.2 tile.39
  287.2 10.1 slice.71
  297.3 12.9 copy.68
  310.2 6.1 slice.72
  316.3 6.6 copy.69
  322.9 48.3 %rev.42 = f32[12,256,512]{1,2,0:T(8,128)} reverse(f32[12,256,512]{1,2,0:T(8,128)} %copy.69), dimensions={2} | reverse | bytes 12582912 | tf_op jit(solution)/shard_map/while/body/eval_jaxpr/while/body/eval_jaxpr/rev | solution.py:40
  393.5 14.2 tile.39
  407.7 10.1 slice.71
  417.8 12.9 copy.68
  430.7 6.1 slice.72
  436.9 6.6 copy.69
  443.5 48.3 %rev.42 = f32[12,256,512]{1,2,0:T(8,128)} reverse(f32[12,256,512]{1,2,0:T(8,128)} %copy.69), dimensions={2} | reverse | bytes 12582912 | tf_op jit(solution)/shard_map/while/body/eval_jaxpr/while/body/eval_jaxpr/rev | solution.py:40
  513.4 6.6 multiply_convert_fusion
  528.6 368.2 %while.61 = (s32[]{:T(128)}, f32[256,12,64]{0,2,1:T(8,128)}, f32[12,32]{1,0:T(8,128)}, bf16[2,512,12,64]{1,3,2,0:T(8,128)(2,1)}, bf16[2,512,12,64]{1,3,2,0:T(8,1...) while((s32[]{:T(128)}, f32[256,12,64]{0,2,1:T(8,128)}, ...), condition=%wide.region_9.10_spmd.clone, body=%wide.region_7.9_spmd.clone.sunk | while | flops 1030591232 | bytes 274231168 | solution.py:269
  563.9 14.2 tile.41
  578.1 10.1 slice.75
  588.2 12.9 copy.70
  601.1 6.1 slice.76
  607.2 6.6 copy.71
  613.7 48.3 %rev.43 = f32[12,256,512]{1,2,0:T(8,128)} reverse(f32[12,256,512]{1,2,0:T(8,128)} %copy.71), dimensions={2} | reverse | bytes 12582912 | tf_op jit(solution)/shard_map/while/body/eval_jaxpr/while/body/eval_jaxpr/rev | solution.py:40
  684.5 4.9 pad_convert_fusion.2
  689.4 20.8 %reshape.329 = f32[12,256,769]{2,1,0:T(8,128)} reshape(f32[12,196864]{1,0:T(8,128)} %pad_convert_fusion.2) | data formatting | bytes 18898944 | tf_op jit(solution)/shard_map/while/body/eval_jaxpr/while/body/eval_jaxpr/reshape | solution.py:56
  710.2 5.5 reduce_sum.141
  733.7 14.2 tile.41
  747.9 10.1 slice.75
  758.0 12.9 copy.70
  770.9 6.1 slice.76
  777.0 6.6 copy.71
  783.6 48.3 %rev.43 = f32[12,256,512]{1,2,0:T(8,128)} reverse(f32[12,256,512]{1,2,0:T(8,128)} %copy.71), dimensions={2} | reverse | bytes 12582912 | tf_op jit(solution)/shard_map/while/body/eval_jaxpr/while/body/eval_jaxpr/rev | solution.py:40
  854.6 4.9 pad_convert_fusion.2
  859.5 20.8 %reshape.329 = f32[12,256,769]{2,1,0:T(8,128)} reshape(f32[12,196864]{1,0:T(8,128)} %pad_convert_fusion.2) | data formatting | bytes 18898944 | tf_op jit(solution)/shard_map/while/body/eval_jaxpr/while/body/eval_jaxpr/reshape | solution.py:56
  880.3 5.5 reduce_sum.141
  913.2 23.5 %reduce-scatter.12.cloned.1.call-done = bf16[1,256,768]{1,2,0:T(8,128)(2,1)} async-done(((bf16[1,1024,768]{1,2,0:T(8,128)(2,1)}), bf16[1,256,768]{1,2,0:T(8,128)(2,1)}) %reduce-scatter.12.cloned.1.call-update) | async-done | bytes 393232 | tf_op jit(solution)/shard_map/reduce_scatter | solution.py:292
  939.9 33.5 %reduce-scatter.10.cloned.1.call-done = bf16[1,256,768]{1,2,0:T(8,128)(2,1)} async-done(((bf16[1,1024,768]{1,2,0:T(8,128)(2,1)}), bf16[1,256,768]{1,2,0:T(8,128)(2,1)}) %reduce-scatter.10.cloned.1.call-update) | async-done | bytes 393232 | tf_op jit(solution)/shard_map/reduce_scatter | solution.py:289
  998.0 39.6 %all-reduce.2 = (f32[768]{0:T(1024)}, f32[768]{0:T(1024)}, f32[32,12]{0,1:T(8,128)}) all-reduce(f32[768]{0:T(1024)S(1)} %get-tuple-element.776, f32[768]{0:T(1024)S(1)} %copy-done.44, f32[32,12]{0,1:T(8,128)S(1)} %bitcast.253), channel_id=1, replica_groups=mesh['dp'=8,'seq'=4] {'dp','seq'}, use_global_device_ids=true, to_apply=%region_21.22 | all-reduce | flops 1920 | bytes 15360 | tf_op jit(solution)/shard_map/psum | solution.py:320
  1038.7 38.5 %reduce-scatter.20.cloned.1.call-done = f32[24,768]{1,0:T(8,128)} async-done(((f32[768,768]{1,0:T(8,128)}), f32[24,768]{1,0:T(8,128)}) %reduce-scatter.20.cloned.1.call-update) | async-done | bytes 73744 | tf_op jit(solution)/shard_map/reduce_scatter | solution.py:314
  1077.2 104.8 %reduce-scatter.14.cloned.1.call-done = f32[24,768]{1,0:T(8,128)} async-done(((f32[768,768]{1,0:T(8,128)}), f32[24,768]{1,0:T(8,128)}) %reduce-scatter.14.cloned.1.call-update) | async-done | bytes 73744 | tf_op jit(solution)/shard_map/reduce_scatter | solution.py:311
  1181.9 103.8 %reduce-scatter.18.cloned.1.call-done = f32[24,768]{1,0:T(8,128)} async-done(((f32[768,768]{1,0:T(8,128)}), f32[24,768]{1,0:T(8,128)}) %reduce-scatter.18.cloned.1.call-update) | async-done | bytes 73744 | tf_op jit(solution)/shard_map/reduce_scatter | solution.py:313
  1285.8 104.6 %reduce-scatter.16.cloned.1.call-done = f32[24,768]{1,0:T(8,128)} async-done(((f32[768,768]{1,0:T(8,128)}), f32[24,768]{1,0:T(8,128)}) %reduce-scatter.16.cloned.1.call-update) | async-done | bytes 73744 | tf_op jit(solution)/shard_map/reduce_scatter | solution.py:312
  1390.3 119.4 %reduce-scatter.26.cloned.1.call-done = f32[64,768]{1,0:T(8,128)} async-done(((f32[2048,768]{1,0:T(8,128)}), f32[64,768]{1,0:T(8,128)}) %reduce-scatter.26.cloned.1.call-update) | async-done | bytes 196624 | tf_op jit(solution)/shard_map/reduce_scatter | solution.py:317
  1509.7 120.6 %reduce-scatter.24.cloned.1.call-done = f32[24,2048]{1,0:T(8,128)} async-done(((f32[768,2048]{1,0:T(8,128)}), f32[24,2048]{1,0:T(8,128)}) %reduce-scatter.24.cloned.1.call-update) | async-done | bytes 196624 | tf_op jit(solution)/shard_map/reduce_scatter | solution.py:316
  1630.3 119.9 %reduce-scatter.22.cloned.1.call-done = f32[24,2048]{1,0:T(8,128)} async-done(((f32[768,2048]{1,0:T(8,128)}), f32[24,2048]{1,0:T(8,128)}) %reduce-scatter.22.cloned.1.call-update) | async-done | bytes 196624 | tf_op jit(solution)/shard_map/reduce_scatter | solution.py:315
  (284 shorter events, 209.7 us)
Async XLA Ops:
  7.2 116.4 %copy-start.8 = (bf16[1,256,768]{2,1,0:T(8,128)(2,1)S(1)}, bf16[1,256,768]{2,1,0:T(8,128)(2,1)}, u32[]{:S(2)}) copy-start(bf16[1,256,768]{2,1,0:T(8,128)(2,1)} %param.18) | copy-start | bytes 1179652
  7.2 116.3 %copy-start.36 = (f32[768]{0:T(1024)S(1)}, f32[768]{0:T(1024)}, u32[]{:S(2)}) copy-start(f32[768]{0:T(1024)} %param.29) | copy-start | bytes 9220
  7.2 60.5 %all-gather.16.cloned.1.call-start = ((), (), s32[]{:S(2)}) async-start(), calls=%async_computation.11 | async-start | bytes 1216512 | tf_op jit(solution)/shard_map/all_gather | solution.py:124
  7.9 115.6 %all-gather.12.cloned.1.call-start = ((), (), s32[]{:S(2)}) async-start(), calls=%async_computation.9 | async-start | bytes 1216512 | tf_op jit(solution)/shard_map/all_gather | solution.py:123
  8.7 170.7 %all-gather.14.cloned.1.call-start = ((), (), s32[]{:S(2)}) async-start(), calls=%async_computation.10 | async-start | bytes 1216512 | tf_op jit(solution)/shard_map/all_gather | solution.py:122
  9.4 207.5 %all-gather.28.cloned.1.call-start = ((), (), s32[]{:S(2)}) async-start(), calls=%async_computation.26 | async-start | bytes 1966080 | tf_op jit(solution)/shard_map/all_gather | solution.py:142
  10.6 115.5 %copy-start.49 = (f32[256]{0:T(256)}, f32[256]{0:T(256)S(1)}, u32[]{:S(2)}) copy-start(f32[256]{0:T(256)S(1)} %fusion.50) | copy-start | bytes 3076
  10.6 168.8 %copy-start.42 = (f32[256]{0:T(256)}, f32[256]{0:T(256)S(1)}, u32[]{:S(2)}) copy-start(f32[256]{0:T(256)S(1)} %fusion.74) | copy-start | bytes 3076
  70.4 184.5 %all-gather.26.cloned.1.call-start = ((), (), s32[]{:S(2)}) async-start(), calls=%async_computation.25 | async-start | bytes 1966080 | tf_op jit(solution)/shard_map/all_gather | solution.py:141
  126.1 374.4 %all-gather.18.cloned.1.call-start = ((), (), s32[]{:S(2)}) async-start(), calls=%async_computation.12 | async-start | bytes 1216512 | tf_op jit(solution)/shard_map/all_gather | solution.py:125
  126.7 378.0 %all-gather.22.cloned.1.call-start = ((), (), s32[]{:S(2)}) async-start(), calls=%async_computation.14 | async-start | bytes 3244032 | tf_op jit(solution)/shard_map/all_gather | solution.py:127
  127.4 381.6 %all-gather.20.cloned.1.call-start = ((), (), s32[]{:S(2)}) async-start(), calls=%async_computation.13 | async-start | bytes 3244032 | tf_op jit(solution)/shard_map/all_gather | solution.py:126
  128.2 385.2 %all-gather.24.cloned.1.call-start = ((), (), s32[]{:S(2)}) async-start(), calls=%async_computation.15 | async-start | bytes 3244032 | tf_op jit(solution)/shard_map/all_gather | solution.py:128
  128.9 807.9 %reduce-scatter.12.cloned.1.call-start = ((), (), s32[]{:S(2)}) async-start(), calls=%async_computation.17 | async-start | bytes 1966080 | tf_op jit(solution)/shard_map/reduce_scatter | solution.py:292
  371.2 4.8 copy-start.5
  491.8 4.8 copy-start.5
  513.4 6.6 copy-start.22
  547.7 16.2 copy-start
  547.7 114.4 %copy-start.2 = (bf16[1024,12,64]{0,2,1:T(8,128)(2,1)}, bf16[1024,12,64]{0,2,1:T(8,128)(2,1)S(1)}, u32[]{:S(2)}) copy-start(bf16[1024,12,64]{0,2,1:T(8,128)(2,1)S(1)} %get-tuple-element.1132) | copy-start | bytes 4718596 | tf_op jit(solution)/shard_map/while/body/eval_jaxpr/while
  613.7 48.3 %copy-start.10 = (pred[256,512]{0,1:T(8,128)(4,1)S(1)}, pred[256,512]{0,1:T(8,128)(4,1)}, u32[]{:S(2)}) copy-start(pred[256,512]{0,1:T(8,128)(4,1)} %broadcast_compare_fusion.5) | copy-start | bytes 393220 | tf_op jit(solution)/shard_map/while/body/eval_jaxpr/while
  662.1 4.6 copy-start.4
  662.1 4.6 copy-start.27
  710.2 5.5 copy-start.39
  710.2 5.5 copy-start.51
  710.2 7.3 copy-start.1
  710.2 7.3 copy-start.3
  717.5 16.2 copy-start
  717.5 114.4 %copy-start.2 = (bf16[1024,12,64]{0,2,1:T(8,128)(2,1)}, bf16[1024,12,64]{0,2,1:T(8,128)(2,1)S(1)}, u32[]{:S(2)}) copy-start(bf16[1024,12,64]{0,2,1:T(8,128)(2,1)S(1)} %get-tuple-element.1132) | copy-start | bytes 4718596 | tf_op jit(solution)/shard_map/while/body/eval_jaxpr/while
  783.6 48.3 %copy-start.10 = (pred[256,512]{0,1:T(8,128)(4,1)S(1)}, pred[256,512]{0,1:T(8,128)(4,1)}, u32[]{:S(2)}) copy-start(pred[256,512]{0,1:T(8,128)(4,1)} %broadcast_compare_fusion.5) | copy-start | bytes 393220 | tf_op jit(solution)/shard_map/while/body/eval_jaxpr/while
  831.9 4.6 copy-start.4
  831.9 4.6 copy-start.27
  880.3 5.5 copy-start.39
  880.3 5.5 copy-start.51
  880.3 7.3 copy-start.1
  880.3 7.3 copy-start.3
  902.3 71.1 %reduce-scatter.10.cloned.1.call-start = ((), (), s32[]{:S(2)}) async-start(), calls=%async_computation.16 | async-start | bytes 1966080 | tf_op jit(solution)/shard_map/reduce_scatter | solution.py:289
  907.8 169.4 %reduce-scatter.20.cloned.1.call-start = ((), (), s32[]{:S(2)}) async-start(), calls=%async_computation.21 | async-start | bytes 2433024 | tf_op jit(solution)/shard_map/reduce_scatter | solution.py:314
  909.8 272.1 %reduce-scatter.14.cloned.1.call-start = ((), (), s32[]{:S(2)}) async-start(), calls=%async_computation.18 | async-start | bytes 2433024 | tf_op jit(solution)/shard_map/reduce_scatter | solution.py:311
  913.2 372.6 %reduce-scatter.18.cloned.1.call-start = ((), (), s32[]{:S(2)}) async-start(), calls=%async_computation.20 | async-start | bytes 2433024 | tf_op jit(solution)/shard_map/reduce_scatter | solution.py:313
  939.8 36.6 %copy-start.23 = (bf16[256,2048]{1,0:T(8,128)(2,1)S(1)}, bf16[256,2048]{1,0:T(8,128)(2,1)}, u32[]{:S(2)}) copy-start(bf16[256,2048]{1,0:T(8,128)(2,1)} %get-tuple-element.841) | copy-start | bytes 3145732
  939.8 36.6 %copy-start.26 = (bf16[1,256,768]{2,1,0:T(8,128)(2,1)S(1)}, bf16[1,256,768]{2,1,0:T(8,128)(2,1)}, u32[]{:S(2)}) copy-start(bf16[1,256,768]{2,1,0:T(8,128)(2,1)} %param.19) | copy-start | bytes 1179652
  939.8 450.5 %reduce-scatter.16.cloned.1.call-start = ((), (), s32[]{:S(2)}) async-start(), calls=%async_computation.19 | async-start | bytes 2433024 | tf_op jit(solution)/shard_map/reduce_scatter | solution.py:312
  976.4 533.4 %reduce-scatter.26.cloned.1.call-start = ((), (), s32[]{:S(2)}) async-start(), calls=%async_computation.24 | async-start | bytes 6488064 | tf_op jit(solution)/shard_map/reduce_scatter | solution.py:317
  980.2 650.1 %reduce-scatter.24.cloned.1.call-start = ((), (), s32[]{:S(2)}) async-start(), calls=%async_computation.23 | async-start | bytes 6488064 | tf_op jit(solution)/shard_map/reduce_scatter | solution.py:316
  985.2 765.0 %reduce-scatter.22.cloned.1.call-start = ((), (), s32[]{:S(2)}) async-start(), calls=%async_computation.22 | async-start | bytes 6488064 | tf_op jit(solution)/shard_map/reduce_scatter | solution.py:315
  992.1 3.8 copy-start.30
  992.1 3.8 copy-start.32
  997.3 40.3 %copy-start.50 = (f32[256]{0:T(256)S(1)}, f32[256]{0:T(256)}, u32[]{:S(2)}) copy-start(f32[256]{0:T(256)} %copy-done.49) | copy-start | bytes 3076
  (39 other events, 59.1 us)
Sparse Core Ops, SparseCore 0:
  10.8 56.7 all-gather.15
  70.5 53.0 all-gather.11
  126.3 53.0 all-gather.13
  180.8 36.0 all-gather.27
  218.9 35.9 all-gather.25
  257.5 52.9 all-gather.17
  313.4 57.9 all-gather.21
  374.3 57.8 all-gather.19
  435.1 57.8 all-gather.23
  902.4 34.2 reduce-scatter.11
  939.1 34.2 reduce-scatter.9
  979.1 98.0 reduce-scatter.19
  1083.9 98.0 reduce-scatter.13
  1187.6 98.0 reduce-scatter.17
  1292.3 97.9 reduce-scatter.15
  1396.4 113.3 reduce-scatter.25
  1516.7 113.5 reduce-scatter.23
  1636.4 113.7 reduce-scatter.21
where the time goes:
time: 1780 us; the launch traced here: 1760 us
  waiting for transfers between devices  1000 us (56%)
  local copies, waits for them, and re-layouts  529 us (30%)
  matrix products  102 us (6%)
  blocking collectives  39.6 us (2%)
  other arithmetic  35 us (2%)
  loops' own time  31.6 us (2%)
    rev x4, local copies, waits for them, and re-layouts, shifted_bias(): return rows[:, :, ::-1]  193 us
    reduce_scatter x1, waiting for transfers between devices, local(): lax.psum_scatter(grad_up, ('dp', 'seq'), scatter_dimension=0, tiled=True)  121 us
    reduce_scatter x1, waiting for transfers between devices, local(): lax.psum_scatter(grad_gate, ('dp', 'seq'), scatter_dimension=0, tiled=True)  120 us
    reduce_scatter x1, waiting for transfers between devices, local(): lax.psum_scatter(grad_down, ('dp', 'seq'), scatter_dimension=0, tiled=True)  119 us
    while x82, local copies, waits for them, and re-layouts  113 us
    reduce_scatter x1, waiting for transfers between devices, local(): lax.psum_scatter(grad_query, ('dp', 'seq'), scatter_dimension=0, tiled=True)  105 us
    reduce_scatter x1, waiting for transfers between devices, local(): lax.psum_scatter(grad_key, ('dp', 'seq'), scatter_dimension=0, tiled=True)  105 us
    reduce_scatter x1, waiting for transfers between devices, local(): lax.psum_scatter(grad_value, ('dp', 'seq'), scatter_dimension=0, tiled=True)  104 us
  transfers between devices with their start and end apart: 18, of which 14 were waited for; matrix products, arithmetic and copies ran while one was open for 17% of the time, Pallas kernels for 0%

commit v1 on v0

--- a/solution.py
+++ b/solution.py
@@ -1,11 +1,16 @@
 import jax
 import jax.numpy as jnp
 from jax import lax
+from jax.experimental import pallas as pl
+from jax.experimental.pallas import tpu as pltpu
 from jax.sharding import PartitionSpec as P
 
 EPS = 1e-06
 MASKED = -1000000000.0
 HIGHEST = lax.Precision.HIGHEST
+GELU_A = 0.7978845608028654
+GELU_B = 0.044715
+VMEM_LIMIT = 56 * 1024 * 1024
 
 
 def norm_rows(values, gain):
@@ -336,9 +341,532 @@
     )
 
 
+def pcall(body, outs, ins, scratch=(), grid=None, in_specs=None, out_specs=None, name=None):
+    kwargs = {}
+    if grid is not None:
+        kwargs = dict(grid=grid, in_specs=in_specs, out_specs=out_specs)
+    else:
+        kwargs = dict(
+            in_specs=[pl.BlockSpec(memory_space=pltpu.SMEM)]
+            + [pl.BlockSpec(memory_space=pltpu.VMEM)] * (len(ins) - 1),
+            out_specs=[pl.BlockSpec(memory_space=pltpu.VMEM)] * len(outs),
+        )
+    return pl.pallas_call(
+        body,
+        out_shape=outs,
+        scratch_shapes=list(scratch),
+        compiler_params=pltpu.CompilerParams(vmem_limit_bytes=VMEM_LIMIT),
+        name=name,
+        **kwargs,
+    )(*ins)
+
+
+def toeplitz(bucket_row, table_col, block):
+    nb = table_col.shape[0]
+    width = bucket_row.shape[1]
+    ids = lax.broadcasted_iota(jnp.int32, (nb, width), 0)
+    per_dist = jnp.sum(jnp.where(bucket_row == ids, table_col, 0.0), axis=0, keepdims=True)
+    return pltpu.roll(
+        jnp.broadcast_to(per_dist, (block, width)), 0, 1, stride=1, stride_axis=0
+    )
+
+
+def diagonals(acc):
+    rows, width = acc.shape
+    while rows > 8:
+        rows //= 2
+        acc = acc[:rows] + pltpu.roll(acc[rows:], width - rows, 1)
+    row = lax.broadcasted_iota(jnp.int32, acc.shape, 0)
+    for bit in (1, 2, 4):
+        acc = jnp.where((row & bit) != 0, pltpu.roll(acc, width - bit, 1), acc)
+    return jnp.sum(acc, axis=0, keepdims=True)
+
+
+def attn_fwd_body(n, heads, head_dim, seq_len, rows):
+    scale = head_dim ** (-0.5)
+
+    def body(z_ref, *refs):
+        x_refs = refs[:n]
+        w_ref, gain_ref, segc_ref, segr_ref, bk_ref, tab_ref = refs[n : n + 6]
+        h1_ref, qkv_ref, o_ref, l_ref = refs[n + 6 : n + 10]
+        piece_refs = refs[n + 10 : 2 * n + 10]
+        toe_ref = refs[2 * n + 10]
+        z = z_ref[0]
+        for k in range(n):
+            start = pl.multiple_of(lax.rem(z + (n - k), n) * rows, rows)
+            xv = x_refs[k][...].astype(jnp.float32)
+            inv = lax.rsqrt(jnp.mean(xv * xv, axis=-1, keepdims=True) + EPS)
+            h1 = (xv * inv * gain_ref[...]).astype(jnp.bfloat16)
+            h1_ref[pl.ds(start, rows), :] = h1
+            qkv = matmul(h1, w_ref[...]).astype(jnp.bfloat16)
+            for i in range(3 * heads):
+                qkv_ref[i, pl.ds(start, rows), :] = qkv[:, i * head_dim : (i + 1) * head_dim]
+        for h in range(heads):
+            toe_ref[h] = toeplitz(bk_ref[...], tab_ref[:, h : h + 1], rows)
+        for k in range(n):
+            start = pl.multiple_of(lax.rem(z + k, n) * rows, rows)
+            seg_q = segc_ref[pl.ds(start, rows), :]
+            outs = []
+            for h in range(heads):
+                s = right_matmul(qkv_ref[h, pl.ds(start, rows), :], qkv_ref[heads + h]) * scale
+                col = pl.multiple_of(seq_len - start, rows)
+                s = s + toe_ref[h, :, pl.ds(col, seq_len)]
+                e = jnp.where(seg_q == segr_ref[...], jnp.exp(s), 0.0)
+                l = jnp.sum(e, axis=-1, keepdims=True)
+                o = matmul(e.astype(jnp.bfloat16), qkv_ref[2 * heads + h]) / l
+                o_ref[h, pl.ds(start, rows), :] = o
+                l_ref[h, pl.ds(start, rows), :] = l
+                outs.append(o)
+            piece_refs[k][...] = jnp.concatenate(outs, axis=1).astype(jnp.bfloat16)
+
+    return body
+
+
+def attn_bwd_body(n, heads, head_dim, seq_len, rows):
+    scale = head_dim ** (-0.5)
+
+    def body(z_ref, *refs):
+        da_refs = refs[:n]
+        h1_ref, qkv_ref, o_ref, l_ref, w_ref = refs[n : n + 5]
+        segc_ref, segr_ref, bk_ref, tab_ref = refs[n + 5 : n + 9]
+        gw_ref, gtab_ref = refs[n + 9 : n + 11]
+        piece_refs = refs[n + 11 : 2 * n + 11]
+        toe_ref, acc_ref, du_ref, dl_ref, dq_ref = refs[2 * n + 11 :]
+        z = z_ref[0]
+        for k in range(n):
+            start = pl.multiple_of(lax.rem(z + (n - k), n) * rows, rows)
+            da = da_refs[k][...].astype(jnp.float32)
+            for h in range(heads):
+                dah = da[:, h * head_dim : (h + 1) * head_dim]
+                l = l_ref[h, pl.ds(start, rows), :]
+                o = o_ref[h, pl.ds(start, rows), :]
+                du_ref[h, pl.ds(start, rows), :] = (dah / l).astype(jnp.bfloat16)
+                dl_ref[h, pl.ds(start, rows), :] = -jnp.sum(dah * o, axis=-1, keepdims=True) / l
+        dq_all, dk_all, dv_all = [], [], []
+        lane = lax.broadcasted_iota(jnp.int32, gtab_ref.shape, 1)
+        gtab = jnp.zeros(gtab_ref.shape, jnp.float32)
+        for h in range(heads):
+            toe_ref[...] = toeplitz(bk_ref[...], tab_ref[:, h : h + 1], rows)
+            acc_ref[...] = jnp.zeros_like(acc_ref)
+            dk = jnp.zeros((head_dim, seq_len), jnp.float32)
+            dv = jnp.zeros((head_dim, seq_len), jnp.float32)
+            for i in range(n):
+                block = pl.ds(i * rows, rows)
+                q = qkv_ref[h, block, :]
+                du = du_ref[h, block, :]
+                cols = pl.ds(seq_len - i * rows, seq_len)
+                s = right_matmul(q, qkv_ref[heads + h]) * scale + toe_ref[:, cols]
+                e = jnp.where(segc_ref[block, :] == segr_ref[...], jnp.exp(s), 0.0)
+                dp = right_matmul(du, qkv_ref[2 * heads + h]) + dl_ref[h, block, :]
+                ds = (e * dp).astype(jnp.bfloat16)
+                acc_ref[:, cols] += ds.astype(jnp.float32)
+                dq = matmul(ds, qkv_ref[heads + h]) * scale
+                dq_ref[block, h * head_dim : (h + 1) * head_dim] = dq.astype(jnp.bfloat16)
+                dk = dk + left_matmul(q, ds)
+                dv = dv + left_matmul(du, e.astype(jnp.bfloat16))
+            first = (heads + h) * head_dim
+            dq_ref[:, first : first + head_dim] = (dk * scale).T.astype(jnp.bfloat16)
+            first = (2 * heads + h) * head_dim
+            dq_ref[:, first : first + head_dim] = dv.T.astype(jnp.bfloat16)
+            sums = diagonals(acc_ref[...])
+            ids = lax.broadcasted_iota(jnp.int32, (gtab_ref.shape[0], sums.shape[1]), 0)
+            col = jnp.sum(jnp.where(bk_ref[...] == ids, sums, 0.0), axis=1, keepdims=True)
+            gtab = gtab + jnp.where(lane == h, col, 0.0)
+        gtab_ref[...] = gtab
+        gw_ref[...] = left_matmul(h1_ref[...], dq_ref[...]).astype(jnp.bfloat16)
+        for k in range(n):
+            start = pl.multiple_of(lax.rem(z + k, n) * rows, rows)
+            part = right_matmul(dq_ref[pl.ds(start, rows), :], w_ref[...])
+            piece_refs[k][...] = part.astype(jnp.bfloat16)
+
+    return body
+
+
+def mid_body(n, rows, width, ff, block, row_w, row_d):
+    steps = ff // block
+    per = block // row_d
+    groups = -(-row_d // row_w)
+    piece_w = width // n
+    off_out = groups * width
+    off_gate = off_out + width
+    off_up = off_gate + ff
+
+    def body(z_ref, *refs):
+        p_refs = refs[:n]
+        x_ref, c_ref, wd_ref, wo_ref, wg_ref, wu_ref, gain_ref = refs[n : n + 7]
+        out_ref, dx1_ref = refs[n + 7 : n + 9]
+        da_refs = refs[n + 9 : 2 * n + 9]
+        gg_ref, grads_ref = refs[2 * n + 9 : 2 * n + 11]
+        x1_s, h2_s, y_s, dh_s, gd_s, go_s, gg_s, gu_s, sems = refs[2 * n + 11 :]
+        z = z_ref[0]
+        j = pl.program_id(0)
+
+        @pl.when(j == 0)
+        def _():
+            x1 = x_ref[...].astype(jnp.float32)
+            for k in range(n):
+                first = pl.multiple_of(lax.rem(z + (n - k), n) * piece_w, piece_w)
+                x1 = x1 + matmul(p_refs[k][...], wo_ref[pl.ds(first, piece_w), :])
+            x1_s[...] = x1
+            inv = lax.rsqrt(jnp.mean(x1 * x1, axis=-1, keepdims=True) + EPS)
+            h2_s[...] = (x1 * inv * gain_ref[...]).astype(jnp.bfloat16)
+            y_s[...] = jnp.zeros_like(y_s)
+            dh_s[...] = jnp.zeros_like(dh_s)
+
+        h2 = h2_s[...]
+        c = c_ref[...]
+        wg = wg_ref[...]
+        wu = wu_ref[...]
+        packed = wd_ref[...].astype(jnp.float32)
+        parts = []
+        for r in range(per):
+            for g in range(groups):
+                size = min(row_w, row_d - g * row_w)
+                parts.append(packed[r * row_w : r * row_w + size, g * width : (g + 1) * width])
+        wd = jnp.concatenate(parts, axis=0).astype(jnp.bfloat16)
+        gate = matmul(h2, wg)
+        up = matmul(h2, wu)
+        t = jnp.tanh(GELU_A * (gate + GELU_B * gate * gate * gate))
+        gelu = 0.5 * gate * (1.0 + t)
+        slope = 0.5 * (1.0 + t) + 0.5 * gate * (1.0 - t * t) * (
+            GELU_A * (1.0 + 3.0 * GELU_B * gate * gate)
+        )
+        hidden = (gelu * up).astype(jnp.bfloat16)
+        y_s[...] += matmul(hidden, wd)
+        dz = right_matmul(c, wd)
+        dgate = (dz * up * slope).astype(jnp.bfloat16)
+        dup = (dz * gelu).astype(jnp.bfloat16)
+        dh_s[...] += right_matmul(dgate, wg) + right_matmul(dup, wu)
+        gdown = left_matmul(hidden, c)
+        rows_out = []
+        for r in range(per):
+            cols_out = []
+            for g in range(groups):
+                size = min(row_w, row_d - g * row_w)
+                first = r * row_d + g * row_w
+                piece = gdown[first : first + size]
+                if size < row_w:
+                    piece = jnp.concatenate(
+                        [piece, jnp.zeros((row_w - size, width), jnp.float32)], axis=0
+                    )
+                cols_out.append(piece)
+            rows_out.append(jnp.concatenate(cols_out, axis=1))
+        gd_s[j] = jnp.concatenate(rows_out, axis=0).astype(jnp.bfloat16)
+        gg_s[j] = left_matmul(h2, dgate).astype(jnp.bfloat16)
+        gu_s[j] = left_matmul(h2, dup).astype(jnp.bfloat16)
+
+        def copies(i):
+            high = per * row_w
+            return (
+                pltpu.make_async_copy(
+                    gd_s.at[i],
+                    grads_ref.at[pl.ds(i * high, high), pl.ds(0, off_out)],
+                    sems.at[0, i],
+                ),
+                pltpu.make_async_copy(
+                    gg_s.at[i],
+                    grads_ref.at[:, pl.ds(off_gate + i * block, block)],
+                    sems.at[1, i],
+                ),
+                pltpu.make_async_copy(
+                    gu_s.at[i],
+                    grads_ref.at[:, pl.ds(off_up + i * block, block)],
+                    sems.at[2, i],
+                ),
+            )
+
+        for copy in copies(j):
+            copy.start()
+
+        @pl.when(j == steps - 1)
+        def _():
+            x1 = x1_s[...]
+            out_ref[...] = (x1 + y_s[...]).astype(jnp.bfloat16)
+            inv = lax.rsqrt(jnp.mean(x1 * x1, axis=-1, keepdims=True) + EPS)
+            hat = x1 * inv
+            dh = dh_s[...]
+            gg_ref[...] = jnp.sum(dh * hat, axis=0, keepdims=True)
+            scaled = dh * gain_ref[...]
+            dxn = inv * (scaled - hat * jnp.mean(scaled * hat, axis=-1, keepdims=True))
+            dx1 = c_ref[...].astype(jnp.float32) + dxn
+            dx1_ref[...] = dx1
+            dy = dx1.astype(jnp.bfloat16)
+            for k in range(n):
+                first = pl.multiple_of(lax.rem(z + k, n) * piece_w, piece_w)
+                da = right_matmul(dy, wo_ref[pl.ds(first, piece_w), :])
+                da_refs[k][...] = da.astype(jnp.bfloat16)
+            for k in range(n):
+                first = pl.multiple_of(lax.rem(z + (n - k), n) * piece_w, piece_w)
+                go_s[pl.ds(first, piece_w), :] = left_matmul(p_refs[k][...], dy).astype(
+                    jnp.bfloat16
+                )
+            last = pltpu.make_async_copy(
+                go_s, grads_ref.at[:, pl.ds(off_out, width)], sems.at[3, 0]
+            )
+            last.start()
+            for i in range(steps):
+                for copy in copies(i):
+                    copy.wait()
+            last.wait()
+
+    return body
+
+
+def final_body(n):
+    def body(z_ref, *refs):
+        part_refs = refs[:n]
+        x_ref, dx1_ref, gain_ref, din_ref, gg_ref = refs[n:]
+        dh = part_refs[0][...].astype(jnp.float32)
+        for k in range(1, n):
+            dh = dh + part_refs[k][...].astype(jnp.float32)
+        xv = x_ref[...].astype(jnp.float32)
+        inv = lax.rsqrt(jnp.mean(xv * xv, axis=-1, keepdims=True) + EPS)
+        hat = xv * inv
+        gg_ref[...] = jnp.sum(dh * hat, axis=0, keepdims=True)
+        scaled = dh * gain_ref[...]
+        dxn = inv * (scaled - hat * jnp.mean(scaled * hat, axis=-1, keepdims=True))
+        din_ref[...] = dx1_ref[...] + dxn
+
+    return body
+
+
+def shifts(pieces, n):
+    got = [pieces[0]]
+    for k in range(1, n):
+        got.append(lax.ppermute(pieces[k], "seq", [(i, (i + k) % n) for i in range(n)]))
+    return got
+
+
+def fast(
+    inputs,
+    d_out,
+    segments,
+    buckets,
+    w_query,
+    w_key,
+    w_value,
+    w_out,
+    w_gate,
+    w_up,
+    w_down,
+    gain_attn,
+    gain_ffn,
+    bias_table,
+):
+    bf16, f32 = jnp.bfloat16, jnp.float32
+    n = lax.axis_size("seq")
+    both = ("dp", "seq")
+    _, rows, width = inputs.shape
+    seq_len = segments.shape[1]
+    nb, head_count = bias_table.shape
+    head_dim = width // head_count
+    heads = head_count // n
+    piece_w = width // n
+    ff = w_gate.shape[1]
+    row_w, row_d = w_query.shape[0], w_down.shape[0]
+    groups = -(-row_d // row_w)
+    z = lax.axis_index("seq")
+    z_arr = jnp.reshape(z, (1,)).astype(jnp.int32)
+    sds = jax.ShapeDtypeStruct
+
+    flat_in = inputs.reshape(rows, width)
+    flat_c = d_out.reshape(rows, width)
+    x_all = shifts([flat_in] * n, n)
+
+    padded = jnp.concatenate([w_down, jnp.zeros((groups * row_w - row_d, width), bf16)], axis=0)
+    down_cols = [padded[g * row_w : (g + 1) * row_w] for g in range(groups)]
+    packed = jnp.concatenate(down_cols + [w_out, w_gate, w_up], axis=1)
+    full = lax.all_gather(packed, both, axis=0, tiled=True)
+
+    three = []
+    for g in range(n):
+        cut = slice(g * piece_w, (g + 1) * piece_w)
+        three += [w_query[:, cut], w_key[:, cut], w_value[:, cut]]
+    own_cols = lax.all_to_all(
+        jnp.concatenate(three, axis=1), "seq", split_axis=1, concat_axis=0, tiled=True
+    )
+    w_qkv = lax.all_gather(own_cols, "dp", axis=0, tiled=True)
+
+    seg_row = segments.reshape(1, seq_len)
+    seg_col = segments.reshape(seq_len, 1)
+    bucket_row = buckets.reshape(1, 2 * seq_len)
+    table = lax.dynamic_slice_in_dim(bias_table, z * heads, heads, axis=1)
+    gain_one = gain_attn.reshape(1, width)
+    gain_two = gain_ffn.reshape(1, width)
+
+    outs = pcall(
+        attn_fwd_body(n, heads, head_dim, seq_len, rows),
+        [
+            sds((seq_len, width), bf16),
+            sds((3 * heads, seq_len, head_dim), bf16),
+            sds((heads, seq_len, head_dim), f32),
+            sds((heads, seq_len, 1), f32),
+        ]
+        + [sds((rows, piece_w), bf16)] * n,
+        [z_arr, *x_all, w_qkv, gain_one, seg_col, seg_row, bucket_row, table],
+        [pltpu.VMEM((heads, rows, 2 * seq_len), f32)],
+        name="attn_fwd",
+    )
+    h1, qkv, o_heads, l_heads = outs[:4]
+    attn = shifts(outs[4:], n)
+
+    block = 256
+    steps = ff // block
+    per = block // row_d
+    const = lambda shape: pl.BlockSpec(shape, lambda j: (0,) * len(shape))
+    total = (groups + 1) * width + 2 * ff
+    gate_first = (groups + 1) * width // block
+    outs = pcall(
+        mid_body(n, rows, width, ff, block, row_w, row_d),
+        [sds((rows, width), bf16), sds((rows, width), f32)]
+        + [sds((rows, piece_w), bf16)] * n
+        + [sds((1, width), f32), sds((width, total), bf16)],
+        [z_arr, *attn, flat_in, flat_c, full, full, full, full, gain_two],
+        [
+            pltpu.VMEM((rows, width), f32),
+            pltpu.VMEM((rows, width), bf16),
+            pltpu.VMEM((rows, width), f32),
+            pltpu.VMEM((rows, width), f32),
+            pltpu.VMEM((steps, per * row_w, groups * width), bf16),
+            pltpu.VMEM((width, width), bf16),
+            pltpu.VMEM((steps, width, block), bf16),
+            pltpu.VMEM((steps, width, block), bf16),
+            pltpu.SemaphoreType.DMA((4, steps)),
+        ],
+        grid=(steps,),
+        in_specs=[pl.BlockSpec(memory_space=pltpu.SMEM)]
+        + [const((rows, piece_w))] * n
+        + [
+            const((rows, width)),
+            const((rows, width)),
+            pl.BlockSpec((per * row_w, groups * width), lambda j: (j, 0)),
+            pl.BlockSpec((width, width), lambda j: (0, groups)),
+            pl.BlockSpec((width, block), lambda j: (0, gate_first + j)),
+            pl.BlockSpec((width, block), lambda j: (0, gate_first + steps + j)),
+            const((1, width)),
+        ],
+        out_specs=[const((rows, width)), const((rows, width))]
+        + [const((rows, piece_w))] * n
+        + [const((1, width)), pl.BlockSpec(memory_space=pl.ANY)],
+        name="mid",
+    )
+    output, dx1 = outs[:2]
+    d_attn = shifts(outs[2 : n + 2], n)
+    gain_two_grad, grads = outs[n + 2 :]
+    reduced = lax.psum_scatter(grads, both, scatter_dimension=0, tiled=True).astype(f32)
+
+    outs = pcall(
+        attn_bwd_body(n, heads, head_dim, seq_len, rows),
+        [sds((width, 3 * piece_w), bf16), sds((nb, 128), f32)] + [sds((rows, width), bf16)] * n,
+        [z_arr, *d_attn, h1, qkv, o_heads, l_heads, w_qkv, seg_col, seg_row, bucket_row, table],
+        [
+            pltpu.VMEM((rows, 2 * seq_len), f32),
+            pltpu.VMEM((rows, 2 * seq_len), f32),
+            pltpu.VMEM((heads, seq_len, head_dim), bf16),
+            pltpu.VMEM((heads, seq_len, 1), f32),
+            pltpu.VMEM((seq_len, 3 * piece_w), bf16),
+        ],
+        name="attn_bwd",
+    )
+    grad_qkv, table_part = outs[:2]
+    d_normed = shifts(outs[2:], n)
+
+    dps = lax.axis_size("dp")
+    spread = lax.all_to_all(grad_qkv, "dp", split_axis=0, concat_axis=0, tiled=True)
+    summed = jnp.sum(spread.reshape(dps, width // dps, 3 * piece_w).astype(f32), axis=0)
+    owned = lax.all_to_all(summed, "seq", split_axis=0, concat_axis=1, tiled=True)
+    owned = owned.reshape(row_w, n, 3, piece_w)
+    grad_query, grad_key, grad_value = (owned[:, :, i].reshape(row_w, width) for i in range(3))
+
+    d_inputs, gain_one_grad = pcall(
+        final_body(n),
+        [sds((rows, width), f32), sds((1, width), f32)],
+        [z_arr, *d_normed, flat_in, dx1, gain_one],
+        name="final",
+    )
+    table_own = lax.dynamic_update_slice_in_dim(
+        jnp.zeros((nb, head_count), f32), table_part[:, :heads], z * heads, axis=1
+    )
+    gain_one_sum, gain_two_sum, table_sum = lax.psum(
+        (gain_one_grad.reshape(width), gain_two_grad.reshape(width), table_own), both
+    )
+
+    base = groups * width
+    down_parts = []
+    for g in range(groups):
+        size = min(row_w, row_d - g * row_w)
+        down_parts.append(reduced[:size, g * width : (g + 1) * width])
+    grad_down = jnp.concatenate(down_parts, axis=0)
+    return (
+        output.reshape(inputs.shape),
+        d_inputs.reshape(inputs.shape),
+        grad_query,
+        grad_key,
+        grad_value,
+        reduced[:, base : base + width],
+        reduced[:, base + width : base + width + ff],
+        reduced[:, base + width + ff :],
+        grad_down,
+        gain_one_sum,
+        gain_two_sum,
+        table_sum,
+    )
+
+
+def pick(
+    inputs,
+    d_out,
+    segments,
+    buckets,
+    w_query,
+    w_key,
+    w_value,
+    w_out,
+    w_gate,
+    w_up,
+    w_down,
+    gain_attn,
+    gain_ffn,
+    bias_table,
+):
+    n = lax.axis_size("seq")
+    seqs, rows, width = inputs.shape
+    row_w, row_d, ff = w_query.shape[0], w_down.shape[0], w_gate.shape[1]
+    head_count = bias_table.shape[1]
+    fits = (
+        seqs == 1
+        and head_count % n == 0
+        and rows == 256
+        and width % 256 == 0
+        and width // head_count == 64
+        and ff % 256 == 0
+        and row_w % 8 == 0
+        and row_d % 8 == 0
+        and 256 % row_d == 0
+        and (256 // row_d) * row_w * (ff // 256) == width
+    )
+    plan = fast if fits else local
+    return plan(
+        inputs,
+        d_out,
+        segments,
+        buckets,
+        w_query,
+        w_key,
+        w_value,
+        w_out,
+        w_gate,
+        w_up,
+        w_down,
+        gain_attn,
+        gain_ffn,
+        bias_table,
+    )
+
+
 def solution(mesh):
     return jax.shard_map(
-        local,
+        pick,
         mesh=mesh,
         in_specs=(
             P("dp", "seq", None),

time: 1780 us -> 336 us (0.19); the launches traced: 1760 us -> 334 us
  waiting for transfers between devices: 1000 us -> 129 us
  local copies, waits for them, and re-layouts: 529 us -> 21.4 us
  matrix products: 102 us -> 0 us
  Pallas kernels: 0 us -> 54.5 us
  blocking collectives: 39.6 us -> 81.6 us
  other arithmetic: 35 us -> 2.26 us
  loops' own time: 31.6 us -> 0 us
  starting transfers between devices: 0.72 us -> 31.1 us
    reduce_scatter x9 -> x1, waiting for transfers between devices: 768 us -> 10.6 us  [fast(): lax.psum_scatter(grads, both, scatter_dimension=0, tiled=True).astype(f32)]
    all_gather x9 -> x1, waiting for transfers between devices: 231 us -> 23.5 us  [fast(): full = lax.all_gather(packed, both, axis=0, tiled=True)]
    rev x4 -> x0, local copies, waits for them, and re-layouts: 193 us -> none  [shifted_bias(): return rows[:, :, ::-1]]
    while x82 -> x0, local copies, waits for them, and re-layouts: 113 us -> none
    dot_general x41 -> x0, matrix products: 102 us -> none  [the longest x7 21.6 us: matmul(): return jnp.dot(left, right, preferred_element_type=jnp.float32)]
    another operation x8 -> x3, local copies, waits for them, and re-layouts: 74 us -> 2.21 us  [fast(): owned[:, :, i].reshape(row_w, width)]
    slice x8 -> x10, local copies, waits for them, and re-layouts: 64.9 us -> 6.08 us  [the longest x2 2.19 us: fast(): down_parts.append(reduced[:size, g * width:(g + 1) * width])]
    pallas_call x0 -> x4, Pallas kernels: none -> 54.5 us  [pcall(): pl.pallas_call(body, out_shape=outs, scratch_shapes=list(scratch), compil...]
  transfers between devices with their start and end apart: 18 -> 17, of which waited for: 14 -> 10; matrix products, arithmetic and copies ran while one was open for 17% -> 3% of each run, Pallas kernels for 0% -> 11%
where the time goes in v1:
time: 336 us; the launch traced here: 334 us
  waiting for transfers between devices  129 us (38%)
  blocking collectives  81.6 us (24%)
  Pallas kernels  54.5 us (16%)
  starting transfers between devices  31.1 us (9%)
  local copies, waits for them, and re-layouts  21.4 us (6%)
  between operations  14.3 us (4%)
    psum x1, blocking collectives, fast(): lax.psum((gain_one_grad.reshape(width), gain_two_grad.reshape(width), tab...  65.5 us
    pallas_call x4, Pallas kernels, pcall(): pl.pallas_call(body, out_shape=outs, scratch_shapes=list(scratch), compil...  54.5 us
    ppermute x12, waiting for transfers between devices, shifts(): lax.ppermute(pieces[k], 'seq', [(i, (i + k) % n) for i in range(n)])  51.1 us
    all_to_all x1, waiting for transfers between devices, fast(): lax.all_to_all(jnp.concatenate(three, axis=1), 'seq', split_axis=1, conca...  34.3 us
    all_gather x1, waiting for transfers between devices, fast(): full = lax.all_gather(packed, both, axis=0, tiled=True)  23.5 us
    ppermute x12, starting transfers between devices, shifts(): lax.ppermute(pieces[k], 'seq', [(i, (i + k) % n) for i in range(n)])  19.8 us
    all_gather x1, blocking collectives, fast(): w_qkv = lax.all_gather(own_cols, 'dp', axis=0, tiled=True)  16.2 us
    reduce_scatter x1, waiting for transfers between devices, fast(): lax.psum_scatter(grads, both, scatter_dimension=0, tiled=True).astype(f32)  10.6 us
  transfers between devices with their start and end apart: 17, of which 10 were waited for; matrix products, arithmetic and copies ran while one was open for 3% of the time, Pallas kernels for 11%

profile of v1, /device:TPU:0, one launch (start us, length us, event | category | flops | bytes accessed | tf_op | source)
XLA Modules:
  0.0 334.3 jit_solution(16316636389497381865)
XLA Ops:
  7.3 0.8 slice_dynamic-update-slice_fusion.1
  8.0 0.8 slice_dynamic-update-slice_fusion
  8.8 0.7 fusion
  9.5 0.8 constant_dynamic-update-slice_fusion.2
  10.3 0.9 constant_dynamic-update-slice_fusion.1
  11.2 0.9 constant_dynamic-update-slice_fusion
  12.1 0.7 copy-done.1
  12.9 3.1 collective-permute-start
  15.9 2.6 collective-permute-start.1
  18.5 1.3 collective-permute-start.2
  19.9 0.9 fusion.4
  20.8 0.9 fusion.6
  22.6 3.3 all-to-all-start
  26.7 1.0 copy.36.refs_6_.refs_9_
  28.3 34.3 %all-to-all-done = bf16[24,4,576]{2,0,1:T(8,128)(2,1)S(1)} async-done(((bf16[24,4,576]{2,0,1:T(8,128)(2,1)}), bf16[24,4,576]{2,0,1:T(8,128)(2,1)S(1)}, u32[]{:S(2)}, u32[]{:S(2)}) %all-to-all-start) | async-done | bytes 110624 | tf_op jit(solution)/shard_map/all_to_all | solution.py:685
  62.7 16.2 %all_gather.6.refs_4_.refs_8_ = bf16[768,576]{1,0:T(8,128)(2,1)} all-gather(bf16[96,576]{1,0:T(8,128)(2,1)S(1)} %bitcast.30), channel_id=1, replica_groups=mesh['dp'=8,'seq'=4] {'dp'}, dimensions={0}, use_global_device_ids=true | all-gather | bytes 995328 | tf_op jit(solution)/shard_map/all_gather | solution.py:688
  78.9 0.7 copy-done.5
  79.9 12.5 %attn_fwd.1 = (bf16[1024,768]{1,0:T(8,128)(2,1)}, bf16[9,1024,64]{2,1,0:T(8,128)(2,1)}, f32[3,1024,64]{2,1,0:T(8,128)}, f32[3,1024,1]{2,1,0:T(8,128)}, bf16[256,...) custom-call(s32[1]{0:T(128)} %bitcast.z_ref, ...), custom_call_target="tpu_custom_call" | custom-call | tf_op jit(solution)/shard_map/attn_fwd/pallas_call | solution.py:354
  92.7 1.8 collective-permute-start.4
  94.5 1.7 collective-permute-start.5
  96.8 6.7 %collective-permute-done.3.refs_1_ = bf16[256,192]{1,0:T(8,128)(2,1)S(1)} collective-permute-done((bf16[256,192]{1,0:T(8,128)(2,1)}, bf16[256,192]{1,0:T(8,128)(2,1)S(1)}, u32[]{:S(2)}, u32[]{:S(2)}) %collective-permute-start.3) | collective-permute-done | bytes 98336 | tf_op jit(solution)/shard_map/ppermute | solution.py:636
  103.6 9.0 %collective-permute-done.4.refs_2_ = bf16[256,192]{1,0:T(8,128)(2,1)S(1)} collective-permute-done((bf16[256,192]{1,0:T(8,128)(2,1)}, bf16[256,192]{1,0:T(8,128)(2,1)S(1)}, u32[]{:S(2)}, u32[]{:S(2)}) %collective-permute-start.4) | collective-permute-done | bytes 98336 | tf_op jit(solution)/shard_map/ppermute | solution.py:636
  112.6 23.5 %all-gather.2.cloned.1.call-done.refs_6_.refs_7_.refs_8_.refs_9_ = bf16[768,7168]{1,0:T(8,128)(2,1)} async-done(((bf16[24,7168]{1,0:T(8,128)(2,1)}), bf16[768,7168]{1,0:T(8,128)(2,1)}) %all-gather.2.cloned.1.call-update) | async-done | bytes 11010064 | tf_op jit(solution)/shard_map/all_gather | solution.py:679
  136.1 19.1 %mid.1 = (bf16[256,768]{1,0:T(8,128)(2,1)}, f32[256,768]{1,0:T(8,128)}, bf16[256,192]{1,0:T(8,128)(2,1)}, bf16[256,192]{1,0:T(8,128)(2,1)}, bf16[256,192]{1,0:T(...) custom-call(s32[1]{0:T(128)} %bitcast.z_ref, ...), custom_call_target="tpu_custom_call" | custom-call | tf_op jit(solution)/shard_map/mid/pallas_call | solution.py:354
  155.2 0.9 copy-done.24
  156.1 1.8 collective-permute-start.7
  158.0 2.0 collective-permute-start.8
  159.9 4.4 %collective-permute-done.6.refs_1_ = bf16[256,192]{1,0:T(8,128)(2,1)S(1)} collective-permute-done((bf16[256,192]{1,0:T(8,128)(2,1)S(1)}, bf16[256,192]{1,0:T(8,128)(2,1)S(1)}, u32[]{:S(2)}, u32[]{:S(2)}) %collective-permute-start.6) | collective-permute-done | bytes 98336 | tf_op jit(solution)/shard_map/ppermute | solution.py:636
  164.3 4.7 %collective-permute-done.7.refs_2_ = bf16[256,192]{1,0:T(8,128)(2,1)S(1)} collective-permute-done((bf16[256,192]{1,0:T(8,128)(2,1)S(1)}, bf16[256,192]{1,0:T(8,128)(2,1)S(1)}, u32[]{:S(2)}, u32[]{:S(2)}) %collective-permute-start.7) | collective-permute-done | bytes 98336 | tf_op jit(solution)/shard_map/ppermute | solution.py:636
  169.7 19.8 %attn_bwd.1 = (bf16[768,576]{1,0:T(8,128)(2,1)}, f32[32,128]{1,0:T(8,128)}, bf16[256,768]{1,0:T(8,128)(2,1)}, bf16[256,768]{1,0:T(8,128)(2,1)}, bf16[256,768]{1,0:T(8,128)(2,1)}, /*index=5*/bf16[256,768]{1,0:T(8,128)(2,1)}) custom-call(s32[1]{0:T(128)} %bitcast.z_ref, bf16[256,192]{1,0:T(8,128)(2,1)} %get-tuple-element.41.refs_0_, ...), custom_call_target="tpu_custom_call" | custom-call | tf_op jit(solution)/shard_map/attn_bwd/pallas_call | solution.py:354
  189.5 3.8 %all-to-all-start.1 = ((bf16[8,96,576]{2,1,0:T(8,128)(2,1)}), bf16[8,96,576]{2,1,0:T(8,128)(2,1)S(1)}, u32[]{:S(2)}, u32[]{:S(2)}) async-start(bf16[8,96,576]{2,1,0:T(8,128)(2,1)} %bitcast.28), calls=%async_computation.1 | async-start | bytes 1966080 | tf_op jit(solution)/shard_map/all_to_all | solution.py:775
  193.4 1.7 collective-permute-start.10
  195.1 3.4 %collective-permute-start.11 = (bf16[256,768]{1,0:T(8,128)(2,1)S(1)}, bf16[256,768]{1,0:T(8,128)(2,1)S(1)}, u32[]{:S(2)}, u32[]{:S(2)}) collective-permute-start(bf16[256,768]{1,0:T(8,128)(2,1)S(1)} %copy-done.20), channel_id=1, source_target_pairs={{0,3},{1,0},{2,1},{3,2},{4,7},{5,4},{6,5},{7,6},{8,11},{9,8},{10,9... | collective-permute-start | bytes 1179656 | tf_op jit(solution)/shard_map/ppermute | solution.py:636
  198.5 9.6 %all-to-all-done.1 = bf16[8,96,576]{2,1,0:T(8,128)(2,1)S(1)} async-done(((bf16[8,96,576]{2,1,0:T(8,128)(2,1)}), bf16[8,96,576]{2,1,0:T(8,128)(2,1)S(1)}, u32[]{:S(2)}, u32[]{:S(2)}) %all-to-all-start.1) | async-done | bytes 884768 | tf_op jit(solution)/shard_map/all_to_all | solution.py:775
  208.1 0.9 convert_reduce_fusion
  208.9 4.1 %all-to-all-start.2 = ((f32[4,24,576]{2,1,0:T(8,128)}), f32[4,24,576]{2,1,0:T(8,128)S(1)}, u32[]{:S(2)}, u32[]{:S(2)}) async-start(f32[4,24,576]{2,1,0:T(8,128)} %bitcast.10), calls=%async_computation.2 | async-start | bytes 491520 | tf_op jit(solution)/shard_map/all_to_all | solution.py:777
  213.2 11.1 %collective-permute-done.10.refs_2_ = bf16[256,768]{1,0:T(8,128)(2,1)S(1)} collective-permute-done((bf16[256,768]{1,0:T(8,128)(2,1)S(1)}, bf16[256,768]{1,0:T(8,128)(2,1)S(1)}, u32[]{:S(2)}, u32[]{:S(2)}) %collective-permute-start.10) | collective-permute-done | bytes 393248 | tf_op jit(solution)/shard_map/ppermute | solution.py:636
  224.3 15.2 %collective-permute-done.9.refs_1_ = bf16[256,768]{1,0:T(8,128)(2,1)S(1)} collective-permute-done((bf16[256,768]{1,0:T(8,128)(2,1)S(1)}, bf16[256,768]{1,0:T(8,128)(2,1)S(1)}, u32[]{:S(2)}, u32[]{:S(2)}) %collective-permute-start.9) | collective-permute-done | bytes 393248 | tf_op jit(solution)/shard_map/ppermute | solution.py:636
  239.6 0.7 copy-done.4
  240.3 3.1 final.1
  244.1 65.5 %all-reduce.1 = (f32[768]{0:T(1024)}, f32[768]{0:T(1024)}, f32[32,12]{0,1:T(8,128)}) all-reduce(f32[768]{0:T(1024)S(1)} %reduce, f32[768]{0:T(1024)S(1)} %reduce.1, f32[32,12]{0,1:T(8,128)S(1)} %dynamic_update_slice.3), channel_id=1, replica_groups=mesh['dp'=8,'seq'=4] {'dp','seq'}, use_global_device_ids=true, to_apply=%region_2.0 | all-reduce | flops 1920 | bytes 15360 | tf_op jit(solution)/shard_map/psum | solution.py:790
  310.0 0.7 reshape_squeeze.10
  310.8 0.7 reshape_squeeze.11
  311.6 0.7 reshape_squeeze.9
  312.3 10.6 %reduce-scatter.2.cloned.1.call-done = bf16[24,7168]{1,0:T(8,128)(2,1)} async-done(((bf16[768,7168]{1,0:T(8,128)(2,1)}), bf16[24,7168]{1,0:T(8,128)(2,1)}) %reduce-scatter.2.cloned.1.call-update) | async-done | bytes 344080 | tf_op jit(solution)/shard_map/reduce_scatter | solution.py:756
  322.9 1.5 fusion.2
  324.4 0.7 slice.108
  325.8 1.7 fusion.3
  (78 shorter events, 6.4 us)
Async XLA Ops:
  7.2 18.8 %copy-start = (f32[32,12]{0,1:T(8,128)S(1)}, f32[32,12]{0,1:T(8,128)}, u32[]{:S(2)}) copy-start(f32[32,12]{0,1:T(8,128)} %param.27) | copy-start | bytes 4612
  7.2 19.5 %copy-start.14 = (s32[1,1024]{1,0:T(1,128)S(1)}, s32[1,1024]{1,0:T(1,128)}, u32[]{:S(2)}) copy-start(s32[1,1024]{1,0:T(1,128)} %refs_10_.1) | copy-start | bytes 12292
  7.2 20.5 %copy-start.16 = (f32[768]{0:T(1024)S(1)}, f32[768]{0:T(1024)}, u32[]{:S(2)}) copy-start(f32[768]{0:T(1024)} %param.25) | copy-start | bytes 9220
  7.2 128.8 %all-gather.2.cloned.1.call-start = ((), (), s32[]{:S(2)}) async-start(), calls=%async_computation.4 | async-start | bytes 11354112 | tf_op jit(solution)/shard_map/all_gather | solution.py:679
  12.1 0.7 copy-start.1
  12.9 66.0 %collective-permute-start = (bf16[256,768]{1,0:T(8,128)(2,1)}, bf16[256,768]{1,0:T(8,128)(2,1)S(1)}, u32[]{:S(2)}, u32[]{:S(2)}) collective-permute-start(bf16[256,768]{1,0:T(8,128)(2,1)} %bitcast.22), channel_id=1, source_target_pairs={{0,1},{1,2},{2,3},{3,0},{4,5},{5,6},{6,7},{7,4},{8,9},{9,10},{10,1... | collective-permute-start | bytes 1179656 | tf_op jit(solution)/shard_map/ppermute | solution.py:636
  15.9 62.9 %collective-permute-start.1 = (bf16[256,768]{1,0:T(8,128)(2,1)}, bf16[256,768]{1,0:T(8,128)(2,1)S(1)}, u32[]{:S(2)}, u32[]{:S(2)}) collective-permute-start(bf16[256,768]{1,0:T(8,128)(2,1)} %bitcast.23), channel_id=1, source_target_pairs={{0,2},{1,3},{2,0},{3,1},{4,6},{5,7},{6,4},{7,5},{8,10},{9,11},{10,... | collective-permute-start | bytes 1179656 | tf_op jit(solution)/shard_map/ppermute | solution.py:636
  18.5 60.3 %collective-permute-start.2 = (bf16[256,768]{1,0:T(8,128)(2,1)}, bf16[256,768]{1,0:T(8,128)(2,1)S(1)}, u32[]{:S(2)}, u32[]{:S(2)}) collective-permute-start(bf16[256,768]{1,0:T(8,128)(2,1)} %bitcast.24), channel_id=1, source_target_pairs={{0,3},{1,0},{2,1},{3,2},{4,7},{5,4},{6,5},{7,6},{8,11},{9,8},{10,9... | collective-permute-start | bytes 1179656 | tf_op jit(solution)/shard_map/ppermute | solution.py:636
  22.6 40.1 %all-to-all-start = ((bf16[24,4,576]{2,0,1:T(8,128)(2,1)}), bf16[24,4,576]{2,0,1:T(8,128)(2,1)S(1)}, u32[]{:S(2)}, u32[]{:S(2)}) async-start(bf16[24,4,576]{2,0,1:T(8,128)(2,1)} %copy.34), calls=%async_computation | async-start | bytes 245760 | tf_op jit(solution)/shard_map/all_to_all | solution.py:685
  25.9 297.0 %reduce-scatter.2.cloned.1.call-start = ((), (), s32[]{:S(2)}) async-start(), calls=%async_computation.5 | async-start | bytes 11354112 | tf_op jit(solution)/shard_map/reduce_scatter | solution.py:756
  62.7 33.6 %copy-start.17 = (f32[768]{0:T(1024)S(1)}, f32[768]{0:T(1024)}, u32[]{:S(2)}) copy-start(f32[768]{0:T(1024)} %param.26) | copy-start | bytes 9220
  78.8 0.7 copy-start.5
  78.8 0.9 copy-start.6
  78.9 1.0 copy-start.7
  92.4 11.2 %collective-permute-start.3 = (bf16[256,192]{1,0:T(8,128)(2,1)}, bf16[256,192]{1,0:T(8,128)(2,1)S(1)}, u32[]{:S(2)}, u32[]{:S(2)}) collective-permute-start(bf16[256,192]{1,0:T(8,128)(2,1)} %get-tuple-element.37), channel_id=1, source_target_pairs={{0,1},{1,2},{2,3},{3,0},{4,5},{5,6},{6,7},{7,4},{8,9},{9,10},{10,1... | collective-permute-start | bytes 294920 | tf_op jit(solution)/shard_map/ppermute | solution.py:636
  92.7 19.9 %collective-permute-start.4 = (bf16[256,192]{1,0:T(8,128)(2,1)}, bf16[256,192]{1,0:T(8,128)(2,1)S(1)}, u32[]{:S(2)}, u32[]{:S(2)}) collective-permute-start(bf16[256,192]{1,0:T(8,128)(2,1)} %get-tuple-element.38), channel_id=1, source_target_pairs={{0,2},{1,3},{2,0},{3,1},{4,6},{5,7},{6,4},{7,5},{8,10},{9,11},{10,... | collective-permute-start | bytes 294920 | tf_op jit(solution)/shard_map/ppermute | solution.py:636
  94.5 18.0 %collective-permute-start.5 = (bf16[256,192]{1,0:T(8,128)(2,1)}, bf16[256,192]{1,0:T(8,128)(2,1)S(1)}, u32[]{:S(2)}, u32[]{:S(2)}) collective-permute-start(bf16[256,192]{1,0:T(8,128)(2,1)} %get-tuple-element.39), channel_id=1, source_target_pairs={{0,3},{1,0},{2,1},{3,2},{4,7},{5,4},{6,5},{7,6},{8,11},{9,8},{10,9... | collective-permute-start | bytes 294920 | tf_op jit(solution)/shard_map/ppermute | solution.py:636
  103.6 32.5 %copy-start.8 = (bf16[256,192]{1,0:T(8,128)(2,1)}, bf16[256,192]{1,0:T(8,128)(2,1)S(1)}, u32[]{:S(2)}) copy-start(bf16[256,192]{1,0:T(8,128)(2,1)S(1)} %collective-permute-done.3.refs_1_) | copy-start | bytes 294916
  112.5 23.5 %copy-start.10 = (bf16[256,192]{1,0:T(8,128)(2,1)}, bf16[256,192]{1,0:T(8,128)(2,1)S(1)}, u32[]{:S(2)}) copy-start(bf16[256,192]{1,0:T(8,128)(2,1)S(1)} %collective-permute-done.4.refs_2_) | copy-start | bytes 294916
  112.5 23.5 %copy-start.12 = (bf16[256,192]{1,0:T(8,128)(2,1)}, bf16[256,192]{1,0:T(8,128)(2,1)S(1)}, u32[]{:S(2)}) copy-start(bf16[256,192]{1,0:T(8,128)(2,1)S(1)} %collective-permute-done.5.refs_3_) | copy-start | bytes 294916
  155.1 0.9 copy-start.24
  155.1 1.0 copy-start.23
  155.1 2.8 copy-start.22
  156.0 8.3 %collective-permute-start.6 = (bf16[256,192]{1,0:T(8,128)(2,1)S(1)}, bf16[256,192]{1,0:T(8,128)(2,1)S(1)}, u32[]{:S(2)}, u32[]{:S(2)}) collective-permute-start(bf16[256,192]{1,0:T(8,128)(2,1)S(1)} %copy-done.24), channel_id=1, source_target_pairs={{0,1},{1,2},{2,3},{3,0},{4,5},{5,6},{6,7},{7,4},{8,9},{9,10},{10,1... | collective-permute-start | bytes 294920 | tf_op jit(solution)/shard_map/ppermute | solution.py:636
  156.1 12.9 %collective-permute-start.7 = (bf16[256,192]{1,0:T(8,128)(2,1)S(1)}, bf16[256,192]{1,0:T(8,128)(2,1)S(1)}, u32[]{:S(2)}, u32[]{:S(2)}) collective-permute-start(bf16[256,192]{1,0:T(8,128)(2,1)S(1)} %copy-done.23), channel_id=1, source_target_pairs={{0,2},{1,3},{2,0},{3,1},{4,6},{5,7},{6,4},{7,5},{8,10},{9,11},{10,... | collective-permute-start | bytes 294920 | tf_op jit(solution)/shard_map/ppermute | solution.py:636
  158.0 11.0 %collective-permute-start.8 = (bf16[256,192]{1,0:T(8,128)(2,1)S(1)}, bf16[256,192]{1,0:T(8,128)(2,1)S(1)}, u32[]{:S(2)}, u32[]{:S(2)}) collective-permute-start(bf16[256,192]{1,0:T(8,128)(2,1)S(1)} %copy-done.22), channel_id=1, source_target_pairs={{0,3},{1,0},{2,1},{3,2},{4,7},{5,4},{6,5},{7,6},{8,11},{9,8},{10,9... | collective-permute-start | bytes 294920 | tf_op jit(solution)/shard_map/ppermute | solution.py:636
  164.3 4.7 %copy-start.9 = (bf16[256,192]{1,0:T(8,128)(2,1)}, bf16[256,192]{1,0:T(8,128)(2,1)S(1)}, u32[]{:S(2)}) copy-start(bf16[256,192]{1,0:T(8,128)(2,1)S(1)} %collective-permute-done.6.refs_1_) | copy-start | bytes 294916
  169.0 0.7 copy-start.11
  169.0 0.7 copy-start.13
  189.5 3.9 %copy-start.21 = (bf16[256,768]{1,0:T(8,128)(2,1)S(1)}, bf16[256,768]{1,0:T(8,128)(2,1)}, u32[]{:S(2)}) copy-start(bf16[256,768]{1,0:T(8,128)(2,1)} %get-tuple-element.51) | copy-start | bytes 1179652
  189.5 5.6 %copy-start.20 = (bf16[256,768]{1,0:T(8,128)(2,1)S(1)}, bf16[256,768]{1,0:T(8,128)(2,1)}, u32[]{:S(2)}) copy-start(bf16[256,768]{1,0:T(8,128)(2,1)} %get-tuple-element.52) | copy-start | bytes 1179652
  189.5 9.0 %copy-start.19 = (bf16[256,768]{1,0:T(8,128)(2,1)S(1)}, bf16[256,768]{1,0:T(8,128)(2,1)}, u32[]{:S(2)}) copy-start(bf16[256,768]{1,0:T(8,128)(2,1)} %get-tuple-element.50) | copy-start | bytes 1179652
  189.5 23.5 %copy-start.18 = (f32[1,768]{1,0:T(1,128)S(1)}, f32[1,768]{1,0:T(1,128)}, u32[]{:S(2)}) copy-start(f32[1,768]{1,0:T(1,128)} %get-tuple-element.58) | copy-start | bytes 9220
  189.5 23.5 %copy-start.15 = (f32[32,128]{1,0:T(8,128)S(1)}, f32[32,128]{1,0:T(8,128)}, u32[]{:S(2)}) copy-start(f32[32,128]{1,0:T(8,128)} %get-tuple-element.59) | copy-start | bytes 49156
  189.5 18.5 %all-to-all-start.1 = ((bf16[8,96,576]{2,1,0:T(8,128)(2,1)}), bf16[8,96,576]{2,1,0:T(8,128)(2,1)S(1)}, u32[]{:S(2)}, u32[]{:S(2)}) async-start(bf16[8,96,576]{2,1,0:T(8,128)(2,1)} %bitcast.28), calls=%async_computation.1 | async-start | bytes 1966080 | tf_op jit(solution)/shard_map/all_to_all | solution.py:775
  193.4 30.9 %collective-permute-start.10 = (bf16[256,768]{1,0:T(8,128)(2,1)S(1)}, bf16[256,768]{1,0:T(8,128)(2,1)S(1)}, u32[]{:S(2)}, u32[]{:S(2)}) collective-permute-start(bf16[256,768]{1,0:T(8,128)(2,1)S(1)} %copy-done.21), channel_id=1, source_target_pairs={{0,2},{1,3},{2,0},{3,1},{4,6},{5,7},{6,4},{7,5},{8,10},{9,11},{10,... | collective-permute-start | bytes 1179656 | tf_op jit(solution)/shard_map/ppermute | solution.py:636
  195.1 29.2 %collective-permute-start.11 = (bf16[256,768]{1,0:T(8,128)(2,1)S(1)}, bf16[256,768]{1,0:T(8,128)(2,1)S(1)}, u32[]{:S(2)}, u32[]{:S(2)}) collective-permute-start(bf16[256,768]{1,0:T(8,128)(2,1)S(1)} %copy-done.20), channel_id=1, source_target_pairs={{0,3},{1,0},{2,1},{3,2},{4,7},{5,4},{6,5},{7,6},{8,11},{9,8},{10,9... | collective-permute-start | bytes 1179656 | tf_op jit(solution)/shard_map/ppermute | solution.py:636
  198.5 41.1 %collective-permute-start.9 = (bf16[256,768]{1,0:T(8,128)(2,1)S(1)}, bf16[256,768]{1,0:T(8,128)(2,1)S(1)}, u32[]{:S(2)}, u32[]{:S(2)}) collective-permute-start(bf16[256,768]{1,0:T(8,128)(2,1)S(1)} %copy-done.19), channel_id=1, source_target_pairs={{0,1},{1,2},{2,3},{3,0},{4,5},{5,6},{6,7},{7,4},{8,9},{9,10},{10,1... | collective-permute-start | bytes 1179656 | tf_op jit(solution)/shard_map/ppermute | solution.py:636
  208.9 100.7 %all-to-all-start.2 = ((f32[4,24,576]{2,1,0:T(8,128)}), f32[4,24,576]{2,1,0:T(8,128)S(1)}, u32[]{:S(2)}, u32[]{:S(2)}) async-start(f32[4,24,576]{2,1,0:T(8,128)} %bitcast.10), calls=%async_computation.2 | async-start | bytes 491520 | tf_op jit(solution)/shard_map/all_to_all | solution.py:777
  224.3 15.2 %copy-start.2 = (bf16[256,768]{1,0:T(8,128)(2,1)}, bf16[256,768]{1,0:T(8,128)(2,1)S(1)}, u32[]{:S(2)}) copy-start(bf16[256,768]{1,0:T(8,128)(2,1)S(1)} %collective-permute-done.10.refs_2_) | copy-start | bytes 1179652
  224.3 15.2 %copy-start.3 = (bf16[256,768]{1,0:T(8,128)(2,1)}, bf16[256,768]{1,0:T(8,128)(2,1)S(1)}, u32[]{:S(2)}) copy-start(bf16[256,768]{1,0:T(8,128)(2,1)S(1)} %collective-permute-done.11.refs_3_) | copy-start | bytes 1179652
  239.6 0.7 copy-start.4
Sparse Core Ops, SparseCore 0:
  13.0 123.0 all-gather.1
  155.3 167.5 reduce-scatter.1
